TPU v7x, 256 devices: a whole 4x4x8 slice. The times are simulated.
256 devices in a mesh: expert: 4 (over y_lo, core), row: 8 (over y_hi, x), col: 8 (over z).
Axes of the slice: x: 4, y: 4 (y_hi: 2, y_lo: 2; y = y_hi * 2 + y_lo), z: 8, core: 2. Of those that a mesh axis runs over, the one named last changes fastest.
Arguments:
- tokens: bfloat16 [512, 2880], P(('expert', 'row'), 'col'), may hold values from -6 to 6
- cotangent: bfloat16 [512, 2880], P(('expert', 'row'), 'col'), may hold values from -6 to 6
- w_gate: bfloat16 [16, 2880, 2880], P('expert', 'col', 'row'), may hold values from -0.109375 to 0.109375
- w_up: bfloat16 [16, 2880, 2880], P('expert', 'col', 'row'), may hold values from -0.109375 to 0.109375
- w_down: bfloat16 [16, 2880, 2880], P('expert', 'row', 'col'), may hold values from -0.109375 to 0.109375
- expert_ids: int32 [512, 4], P(('expert', 'row')), may hold values from 0 to 15, all different within a row; in each aligned block of 16 rows (0 to 15, 16 to 31, ...) at most 8 rows name the same one
- gates: float32 [512, 4], P(('expert', 'row')), may hold values from 0.05 to 1
Outputs:
- mixed: bfloat16 [512, 2880], P(('expert', 'row'), 'col')
- d_tokens: bfloat16 [512, 2880], P(('expert', 'row'), 'col')
- d_gates: float32 [512, 4], P(('expert', 'row'))
- grad_gate: bfloat16 [16, 2880, 2880], P('expert', 'col', 'row')
- grad_up: bfloat16 [16, 2880, 2880], P('expert', 'col', 'row')
- grad_down: bfloat16 [16, 2880, 2880], P('expert', 'row', 'col')
Inputs may be any that keep to these rules, and one draw needn't show every extreme that they name: `expert_ids`: the 4 experts of a token are distinct. Within one token block of 16 consecutive tokens no expert is chosen by more than 8 pairs, and some expert is chosen by exactly 8 pairs in some blocks.
All inputs are finite; a program needn't handle non-finite values.
Results may differ from a plain program's by a relative error of at most 0.0058.
Values may be sent and summed in bfloat16 or wider, within the bound.
No kernel may reach another device: no remote copies, remote signals or barrier semaphores. Data moves between devices by JAX's collectives and lax.ppermute only.
A program may use at most 128 MiB of HBM per device.

v0:
```python
import jax
import jax.numpy as jnp
from jax import lax
from jax.sharding import PartitionSpec as P

TOPK = 4
EXP_GROUP = 4
CAP = 8


def sent_to_all(value, axis):
    peers = lax.axis_size(axis)
    return lax.all_to_all(
        jnp.broadcast_to(value[None], (peers, *value.shape)), axis, 0, 0, tiled=True
    )


def laid_out(pieces, dim):
    pieces = jnp.moveaxis(pieces, 0, dim)
    lengths = pieces.shape
    return pieces.reshape(*lengths[:dim], lengths[dim] * lengths[dim + 1], *lengths[dim + 2 :])


def gathered_copies(value, axis, dim):
    pieces = sent_to_all(value, axis)
    return laid_out(pieces, dim)


def sent_together(arrays, axis, split_dim, concat_dim, along):
    ends, at = ([], 0)
    for a in arrays[:-1]:
        at += a.shape[along]
        ends.append(at)
    both = jnp.concatenate(arrays, axis=along)
    return tuple(
        jnp.split(
            lax.all_to_all(both, axis, split_axis=split_dim, concat_axis=concat_dim, tiled=True),
            ends,
            axis=along,
        )
    )


def taken_together(value, axis):
    return sent_to_all(value, axis).sum(axis=0)


def local(tokens, cotangent, w_gate, w_up, w_down, expert_ids, gates):
    n_groups = lax.axis_size("expert")
    tok_count = tokens.shape[0]
    feat_width = tokens.shape[1]
    expert_count = EXP_GROUP * n_groups
    slot_total = expert_count * CAP
    flat_ids = expert_ids.reshape(-1)
    onehot = (flat_ids[:, None] == jnp.arange(expert_count, dtype=jnp.int32)[None, :]).astype(
        jnp.int32
    )
    slot = jnp.sum((jnp.cumsum(onehot, axis=0) - onehot) * onehot, axis=1).reshape(tok_count, TOPK)
    position = (
        expert_ids // EXP_GROUP * (CAP * EXP_GROUP) + slot * EXP_GROUP + expert_ids % EXP_GROUP
    )
    picker = (
        position[:, :, None] == jnp.arange(slot_total, dtype=jnp.int32)[None, None, :]
    ).astype(jnp.float32)
    weighted = jnp.sum(picker * gates[:, :, None], axis=1)
    chosen = jnp.sum(picker, axis=1).astype(jnp.bfloat16)
    x_buffer = jnp.einsum("tp,td->pd", chosen, tokens, preferred_element_type=jnp.float32).astype(
        jnp.bfloat16
    )
    dy_buffer = jnp.einsum(
        "tp,td->pd", weighted, cotangent.astype(jnp.float32), precision=lax.Precision.HIGHEST
    )
    x_buffer = x_buffer.reshape(n_groups, CAP, EXP_GROUP, feat_width)
    dy_buffer = dy_buffer.reshape(n_groups, CAP, EXP_GROUP, feat_width)
    x_local = lax.all_to_all(x_buffer, "expert", split_axis=0, concat_axis=1, tiled=True)
    dy_local = lax.all_to_all(dy_buffer, "expert", split_axis=0, concat_axis=1, tiled=True)
    x_local = x_local.reshape(n_groups * CAP, EXP_GROUP, feat_width)
    dy_local = dy_local.reshape(n_groups * CAP, EXP_GROUP, feat_width)
    x_full = gathered_copies(x_local, "row", 0)
    dy_full = gathered_copies(dy_local, "row", 0)
    down_wide = w_down.astype(jnp.float32)
    gate_part = jnp.einsum("mek,ekf->mef", x_full, w_gate, preferred_element_type=jnp.float32)
    up_part = jnp.einsum("mek,ekf->mef", x_full, w_up, preferred_element_type=jnp.float32)
    both_sums = lax.psum(jnp.stack([gate_part, up_part], axis=2), "col")
    gate_pre = both_sums[:, :, 0]
    up_pre = both_sums[:, :, 1]
    sigma_gate = jax.nn.sigmoid(gate_pre)
    hidden = (gate_pre * sigma_gate * up_pre).astype(jnp.bfloat16)
    gate_pre, up_pre, sigma_gate, hidden_full = (gate_pre, up_pre, sigma_gate, hidden)
    y_local = lax.psum_scatter(
        jnp.einsum("mef,efd->med", hidden_full, w_down, preferred_element_type=jnp.float32),
        "row",
        scatter_dimension=0,
        tiled=True,
    ).astype(jnp.bfloat16)
    grad_hidden = lax.psum(
        jnp.einsum("med,efd->mef", dy_full, down_wide, precision=lax.Precision.HIGHEST), "col"
    )
    grad_gate_pre = grad_hidden * up_pre * sigma_gate * (1.0 + gate_pre * (1.0 - sigma_gate))
    grad_up_pre = grad_hidden * gate_pre * sigma_gate
    grad_pair = jnp.stack([grad_gate_pre, grad_up_pre], axis=2).astype(jnp.bfloat16)
    from_gate = jnp.einsum(
        "mef,ekf->mek", grad_pair[:, :, 0], w_gate, preferred_element_type=jnp.float32
    )
    from_up = jnp.einsum(
        "mef,ekf->mek", grad_pair[:, :, 1], w_up, preferred_element_type=jnp.float32
    )
    dx_local = lax.psum_scatter(from_gate + from_up, "row", scatter_dimension=0, tiled=True).astype(
        jnp.bfloat16
    )
    grad_gate = jnp.einsum(
        "mek,mef->ekf", x_full, grad_pair[:, :, 0], preferred_element_type=jnp.float32
    ).astype(jnp.bfloat16)
    grad_up = jnp.einsum(
        "mek,mef->ekf", x_full, grad_pair[:, :, 1], preferred_element_type=jnp.float32
    ).astype(jnp.bfloat16)
    grad_down = jnp.einsum(
        "mef,med->efd", hidden_full.astype(jnp.float32), dy_full, precision=lax.Precision.HIGHEST
    ).astype(jnp.bfloat16)
    y_send = y_local.reshape(n_groups, CAP, EXP_GROUP, feat_width)
    dx_send = dx_local.reshape(n_groups, CAP, EXP_GROUP, feat_width)
    y_back, dx_back = sent_together((y_send, dx_send), "expert", 0, 0, 1)
    y_back = y_back.reshape(slot_total, feat_width)
    dx_back = dx_back.reshape(slot_total, feat_width)
    y_pairs = jnp.einsum(
        "tkp,pd->tkd", picker.astype(jnp.bfloat16), y_back, preferred_element_type=jnp.float32
    )
    mixed = jnp.sum(gates[:, :, None] * y_pairs, axis=1).astype(jnp.bfloat16)
    d_tokens = jnp.einsum("tp,pd->td", chosen, dx_back, preferred_element_type=jnp.float32).astype(
        jnp.bfloat16
    )
    gate_terms = jnp.sum(cotangent.astype(jnp.float32)[:, None, :] * y_pairs, axis=2)
    d_gates = taken_together(gate_terms, "col")
    return (mixed, d_tokens, d_gates, grad_gate, grad_up, grad_down)


def solution(mesh):
    in_specs = (
        P(("expert", "row"), "col"),
        P(("expert", "row"), "col"),
        P("expert", "col", "row"),
        P("expert", "col", "row"),
        P("expert", "row", "col"),
        P(("expert", "row"), None),
        P(("expert", "row"), None),
    )
    out_specs = (
        P(("expert", "row"), "col"),
        P(("expert", "row"), "col"),
        P(("expert", "row"), None),
        P("expert", "col", "row"),
        P("expert", "col", "row"),
        P("expert", "row", "col"),
    )
    return jax.shard_map(local, mesh=mesh, in_specs=in_specs, out_specs=out_specs, check_vma=False)
```

profile of v0, /device:TPU:1, one launch (start us, length us, event | category | flops | bytes accessed | tf_op | source)
XLA Modules:
  0.0 331.1 jit_solution(17469069092715718256)
XLA Ops:
  7.2 0.0 copy-start
  7.2 0.8 copy.48
  8.0 0.1 eq.30
  8.1 0.1 fusion.6
  8.2 0.1 reduce_window_sum.11
  8.3 0.2 select_reduce_fusion.1
  8.5 0.1 mul.69
  8.6 0.1 copy.53
  8.7 0.8 convert_reduce_fusion
  9.5 1.0 convolution_convert_fusion.3
  10.4 0.1 copy.54
  10.6 0.7 reshape.53
  11.2 6.5 %all-to-all-start = ((bf16[4,8,4,360]{3,2,1,0:T(4,128)(2,1)}), bf16[4,8,4,360]{3,2,1,0:T(4,128)(2,1)S(1)}, u32[]{:S(2)}, u32[]{:S(2)}) async-start(bf16[4,8,4,360]{3,2,1,0:T(4,128)(2,1)} %reshape.53), calls=%async_computation | async-start | bytes 196608 | tf_op jit(solution)/shard_map/all_to_all | solution.py:75
  17.7 0.1 copy.64
  17.8 1.6 fusion.4
  19.4 1.7 all-to-all-done
  21.1 4.3 %all-to-all-start.2 = ((f32[4,8,4,360]{3,1,2,0:T(8,128)}), f32[4,8,4,360]{3,1,2,0:T(8,128)S(1)}, u32[]{:S(2)}, u32[]{:S(2)}) async-start(f32[4,8,4,360]{3,1,2,0:T(8,128)} %fusion.4), calls=%async_computation.2 | async-start | bytes 393216 | tf_op jit(solution)/shard_map/all_to_all | solution.py:76
  25.4 4.1 %all-to-all-done.2 = f32[4,8,4,360]{3,1,2,0:T(8,128)S(1)} async-done(((f32[4,8,4,360]{3,1,2,0:T(8,128)}), f32[4,8,4,360]{3,1,2,0:T(8,128)S(1)}, u32[]{:S(2)}, u32[]{:S(2)}) %all-to-all-start.2) | async-done | bytes 184352 | tf_op jit(solution)/shard_map/all_to_all | solution.py:76
  29.4 1.0 broadcast_in_dim.11
  30.4 4.9 %all-to-all-start.1 = ((bf16[8,32,4,360]{3,1,2,0:T(8,128)(2,1)}), bf16[8,32,4,360]{3,1,2,0:T(8,128)(2,1)S(1)}, u32[]{:S(2)}, u32[]{:S(2)}) async-start(bf16[8,32,4,360]{3,1,2,0:T(8,128)(2,1)} %broadcast_in_dim.11), calls=%async_computation.1 | async-start | bytes 1572864 | tf_op jit(solution)/shard_map/all_to_all | solution.py:13
  35.4 14.5 %all-to-all-done.1 = bf16[8,32,4,360]{3,1,2,0:T(8,128)(2,1)S(1)} async-done(((bf16[8,32,4,360]{3,1,2,0:T(8,128)(2,1)}), bf16[8,32,4,360]{3,1,2,0:T(8,128)(2,1)S(1)}, u32[]{:S(2)}, u32[]{:S(2)}) %all-to-all-start.1) | async-done | bytes 737312 | tf_op jit(solution)/shard_map/all_to_all | solution.py:13
  49.9 1.4 broadcast_in_dim.13
  51.4 0.0 copy-done.7
  51.4 4.3 %all-to-all-start.3 = ((f32[8,32,4,360]{3,1,2,0:T(8,128)}), f32[8,32,4,360]{3,1,2,0:T(8,128)}, u32[]{:S(2)}, u32[]{:S(2)}) async-start(f32[8,32,4,360]{3,1,2,0:T(8,128)} %broadcast_in_dim.13), calls=%async_computation.3 | async-start | bytes 3145728 | tf_op jit(solution)/shard_map/all_to_all | solution.py:13
  55.7 0.0 copy-start.5
  55.7 0.0 all-reduce.7.cloned.1.call-start
  55.7 1.3 copy.56
  57.0 0.1 copy-done.5
  57.2 0.6 convolution_bitcast_fusion.2
  57.8 0.6 copy-done.3
  58.4 0.6 convolution_bitcast_fusion.3
  59.0 1.9 pad_maximum_fusion
  60.9 17.8 %all-to-all-done.3 = f32[8,32,4,360]{3,1,2,0:T(8,128)} async-done(((f32[8,32,4,360]{3,1,2,0:T(8,128)}), f32[8,32,4,360]{3,1,2,0:T(8,128)}, u32[]{:S(2)}, u32[]{:S(2)}) %all-to-all-start.3) | async-done | bytes 1474592 | tf_op jit(solution)/shard_map/all_to_all | solution.py:13
  78.7 1.5 copy.67
  80.2 0.0 copy-done
  80.2 2.6 convolution_bitcast_fusion
  82.9 0.0 all-reduce.7.cloned.1.call-update
  82.9 0.7 copy-done.8
  83.6 0.0 copy-done.10
  83.6 0.6 dynamic-slice
  84.8 111.1 %all-reduce.7.cloned.1.call-done = (f32[256,4,360]{0,2,1:T(8,128)}, f32[256,4,2,360]{0,3,1,2:T(8,128)}) async-done(((f32[256,4,360]{0,2,1:T(8,128)}, f32[256,4,2,360]{0,3,1,2:T(8,128)}), (f32[256,4,360]{0,2,1:T(8,128)}, f32[256,4,2,360]{0,3,1,2:T(8,128)})) %all-reduce.7.cloned.1.call-update) | async-done | bytes 4423696 | tf_op jit(solution)/shard_map/psum | solution.py:96
  195.9 3.0 multiply_convert_fusion
  198.9 1.8 convolution_bitcast_fusion.1
  200.7 2.4 convolution_convert_fusion
  203.1 0.6 fusion.19
  203.6 0.0 copy-start.6
  203.7 1.7 convolution_convert_fusion.1
  205.3 1.7 add_bitcast_fusion
  207.0 1.8 copy.69
  208.8 2.6 copy.62
  211.4 78.4 %all-reduce.8 = (bf16[256,4,360]{2,1,0:T(4,128)(2,1)}, bf16[256,4,360]{2,1,0:T(4,128)(2,1)}) all-reduce(f32[256,4,360]{2,1,0:T(4,128)S(1)} %copy.69, f32[256,4,360]{2,1,0:T(4,128)} %copy.62), channel_id=3, replica_groups=mesh['expert'=4,'row'=8,'col'=8] {'row'}, use_global_device_ids=true, to_apply=%region_7.8.clone | all-reduce | flops 737280 | bytes 4423680
  289.8 1.1 constant_dynamic-slice_fusion
  291.0 0.7 copy.71
  291.7 15.2 %all-to-all-start.4 = ((bf16[4,16,4,360]{3,1,2,0:T(8,128)(2,1)}), bf16[4,16,4,360]{3,1,2,0:T(8,128)(2,1)S(1)}, u32[]{:S(2)}, u32[]{:S(2)}) async-start(bf16[4,16,4,360]{3,1,2,0:T(8,128)(2,1)} %copy.71), calls=%async_computation.4 | async-start | bytes 393216 | tf_op jit(solution)/shard_map/all_to_all | solution.py:37
  306.9 1.7 convolution_convert_fusion.2
  308.6 2.4 all-to-all-done.4
  311.1 0.1 reshape.59
  311.2 0.1 reshape.58
  311.2 0.8 multiply_reduce_fusion
  312.1 0.6 broadcast_in_dim.14
  312.7 4.3 %all-to-all-start.5 = ((f32[8,16,4]{1,2,0:T(4,128)}), f32[8,16,4]{1,2,0:T(4,128)S(1)}, u32[]{:S(2)}, u32[]{:S(2)}) async-start(f32[8,16,4]{1,2,0:T(4,128)} %broadcast_in_dim.14), calls=%async_computation.5 | async-start | bytes 32768 | tf_op jit(solution)/shard_map/all_to_all | solution.py:13
  317.0 0.7 convolution_convert_fusion.4
  317.7 5.9 %all-to-all-done.5 = f32[8,16,4]{1,2,0:T(4,128)S(1)} async-done(((f32[8,16,4]{1,2,0:T(4,128)}), f32[8,16,4]{1,2,0:T(4,128)S(1)}, u32[]{:S(2)}, u32[]{:S(2)}) %all-to-all-start.5) | async-done | bytes 2080 | tf_op jit(solution)/shard_map/all_to_all | solution.py:13
  323.6 0.6 reduce_sum.59
  (24 shorter events, 0.2 us)
Async XLA Ops:
  7.2 73.1 %copy-start = (bf16[4,360,360]{2,1,0:T(8,128)(2,1)S(1)}, bf16[4,360,360]{2,1,0:T(8,128)(2,1)}, u32[]{:S(2)}) copy-start(bf16[4,360,360]{2,1,0:T(8,128)(2,1)} %param.11) | copy-start | bytes 3110404
  11.2 9.8 %all-to-all-start = ((bf16[4,8,4,360]{3,2,1,0:T(4,128)(2,1)}), bf16[4,8,4,360]{3,2,1,0:T(4,128)(2,1)S(1)}, u32[]{:S(2)}, u32[]{:S(2)}) async-start(bf16[4,8,4,360]{3,2,1,0:T(4,128)(2,1)} %reshape.53), calls=%async_computation | async-start | bytes 196608 | tf_op jit(solution)/shard_map/all_to_all | solution.py:75
  21.1 8.4 %all-to-all-start.2 = ((f32[4,8,4,360]{3,1,2,0:T(8,128)}), f32[4,8,4,360]{3,1,2,0:T(8,128)S(1)}, u32[]{:S(2)}, u32[]{:S(2)}) async-start(f32[4,8,4,360]{3,1,2,0:T(8,128)} %fusion.4), calls=%async_computation.2 | async-start | bytes 393216 | tf_op jit(solution)/shard_map/all_to_all | solution.py:76
  30.4 19.5 %all-to-all-start.1 = ((bf16[8,32,4,360]{3,1,2,0:T(8,128)(2,1)}), bf16[8,32,4,360]{3,1,2,0:T(8,128)(2,1)S(1)}, u32[]{:S(2)}, u32[]{:S(2)}) async-start(bf16[8,32,4,360]{3,1,2,0:T(8,128)(2,1)} %broadcast_in_dim.11), calls=%async_computation.1 | async-start | bytes 1572864 | tf_op jit(solution)/shard_map/all_to_all | solution.py:13
  49.9 1.4 copy-start.7
  51.4 27.3 %all-to-all-start.3 = ((f32[8,32,4,360]{3,1,2,0:T(8,128)}), f32[8,32,4,360]{3,1,2,0:T(8,128)}, u32[]{:S(2)}, u32[]{:S(2)}) async-start(f32[8,32,4,360]{3,1,2,0:T(8,128)} %broadcast_in_dim.13), calls=%async_computation.3 | async-start | bytes 3145728 | tf_op jit(solution)/shard_map/all_to_all | solution.py:13
  55.7 1.5 copy-start.5
  55.7 140.2 %all-reduce.7.cloned.1.call-start = ((), (), s32[]{:S(2)}) async-start(), calls=%async_computation.6 | async-start | bytes 8847360 | tf_op jit(solution)/shard_map/psum | solution.py:96
  57.2 1.2 copy-start.3
  82.9 0.7 copy-start.8
  82.9 0.7 copy-start.10
  198.9 4.1 %copy-start.1 = (bf16[256,4,360]{0,2,1:T(8,128)(2,1)}, bf16[256,4,360]{0,2,1:T(8,128)(2,1)S(1)}, u32[]{:S(2)}) copy-start(bf16[256,4,360]{0,2,1:T(8,128)(2,1)S(1)} %get-tuple-element.15) | copy-start | bytes 2211844
  200.7 2.4 copy-start.4
  203.6 1.7 copy-start.6
  289.8 17.1 %copy-start.2 = (bf16[256,4,360]{0,2,1:T(8,128)(2,1)S(1)}, bf16[256,4,360]{0,2,1:T(8,128)(2,1)}, u32[]{:S(2)}) copy-start(bf16[256,4,360]{0,2,1:T(8,128)(2,1)} %copy-done.1) | copy-start | bytes 2211844
  291.7 19.3 %all-to-all-start.4 = ((bf16[4,16,4,360]{3,1,2,0:T(8,128)(2,1)}), bf16[4,16,4,360]{3,1,2,0:T(8,128)(2,1)S(1)}, u32[]{:S(2)}, u32[]{:S(2)}) async-start(bf16[4,16,4,360]{3,1,2,0:T(8,128)(2,1)} %copy.71), calls=%async_computation.4 | async-start | bytes 393216 | tf_op jit(solution)/shard_map/all_to_all | solution.py:37
  306.9 4.3 %copy-start.9 = (f32[16,4]{0,1:T(4,128)S(1)}, f32[16,4]{0,1:T(4,128)}, u32[]{:S(2)}) copy-start(f32[16,4]{0,1:T(4,128)} %param.13) | copy-start | bytes 772
  312.7 11.0 %all-to-all-start.5 = ((f32[8,16,4]{1,2,0:T(4,128)}), f32[8,16,4]{1,2,0:T(4,128)S(1)}, u32[]{:S(2)}, u32[]{:S(2)}) async-start(f32[8,16,4]{1,2,0:T(4,128)} %broadcast_in_dim.14), calls=%async_computation.5 | async-start | bytes 32768 | tf_op jit(solution)/shard_map/all_to_all | solution.py:13
Sparse Core Ops, SparseCore 0:
  83.0 112.8 all-reduce.6
where the time goes:
time: 332 us; the launch traced here: 331 us
  waiting for transfers between devices  157 us (47%)
  blocking collectives  78.4 us (24%)
  starting transfers between devices  39.6 us (12%)
  matrix products  17.7 us (5%)
  local copies, waits for them, and re-layouts  16.3 us (5%)
  between operations  14.9 us (4%)
  other arithmetic  6.7 us (2%)
    psum x1, waiting for transfers between devices, local(): lax.psum(jnp.einsum('med,efd->mef', dy_full, down_wide, precision=lax.Pre...  111 us
    unnamed x1, blocking collectives  78.4 us
    all_to_all x3, waiting for transfers between devices, sent_to_all(): lax.all_to_all(jnp.broadcast_to(value[None], (peers, *value.shape)), axis...  38.2 us
    all_to_all x1, starting transfers between devices, sent_together(): lax.all_to_all(both, axis, split_axis=split_dim, concat_axis=concat_dim,...  15.2 us
    all_to_all x3, starting transfers between devices, sent_to_all(): lax.all_to_all(jnp.broadcast_to(value[None], (peers, *value.shape)), axis...  13.6 us
  transfers between devices with their start and end apart: 7, of which 7 were waited for; matrix products, arithmetic and copies ran while one was open for 3% of the time, Pallas kernels for 0%

commit v1 on v0

v1 whole, which is shorter than its diff:
```python
import jax
import jax.numpy as jnp
from jax import lax
from jax.sharding import PartitionSpec as P

TOPK = 4
EXP_GROUP = 4
PLANE = ("expert", "row")
F32 = jnp.float32
BF16 = jnp.bfloat16


def narrowed(value):
    return lax.reduce_precision(value, 8, 7)


def in_parts(value, count):
    parts = []
    for _ in range(count):
        top = narrowed(value)
        parts.append(top.astype(BF16))
        value = value - top
    return parts


def told_to_all(value, axis):
    peers = lax.axis_size(axis)
    return lax.all_to_all(
        jnp.broadcast_to(value[None], (peers, *value.shape)), axis, 0, 0, tiled=True
    )


def dispatched(tokens, cotangent, expert_ids, gates):
    width = tokens.shape[1]
    own = jnp.concatenate(
        [tokens, cotangent, expert_ids.astype(BF16), *in_parts(gates, 3)], axis=1
    )
    every = told_to_all(own, PLANE)
    every = every.reshape(-1, own.shape[1])
    ids = every[:, 2 * width : 2 * width + TOPK].astype(jnp.int32)
    parts = every[:, 2 * width + TOPK :].astype(F32)
    weights = parts[:, :TOPK] + parts[:, TOPK : 2 * TOPK] + parts[:, 2 * TOPK :]
    return every[:, :width], every[:, width : 2 * width], ids, weights


def routed(rows, tok_all, cot_all, match, gate_of, place, w_gate, w_up, w_down):
    chunks = lax.axis_size("col")
    chunk = rows // chunks
    ff = w_gate.shape[2]
    row_ids = jnp.arange(rows, dtype=jnp.int32)
    picks = jnp.stack([(place[:, e][None, :] == row_ids[:, None]) for e in range(EXP_GROUP)])
    pick_bf = picks.astype(BF16)
    both = jnp.concatenate([tok_all, cot_all], axis=1)
    spread = jnp.einsum("ert,td->erd", pick_bf, both, preferred_element_type=F32).astype(BF16)
    width = tok_all.shape[1]
    x_rows, c_rows = spread[:, :, :width], spread[:, :, width:]
    gate_part = jnp.einsum("erd,edf->rf", x_rows, w_gate, preferred_element_type=F32)
    up_part = jnp.einsum("erd,edf->rf", x_rows, w_up, preferred_element_type=F32)
    dh_part = jnp.einsum("erd,efd->rf", c_rows, w_down, preferred_element_type=F32)
    parts = jnp.concatenate([gate_part, up_part, dh_part], axis=1).astype(BF16)
    pieces = lax.all_to_all(parts.reshape(chunks, chunk, 3 * ff), "col", 0, 0, tiled=True)
    sums = jnp.sum(pieces.astype(F32), axis=0)
    gate_pre, up_pre, dh_raw = sums[:, :ff], sums[:, ff : 2 * ff], sums[:, 2 * ff :]
    mine = lax.axis_index("col") * chunk + jnp.arange(chunk, dtype=jnp.int32)
    row_gate = sum(
        jnp.sum(
            jnp.where(place[:, e][None, :] == mine[:, None], gate_of[:, e][None, :], 0.0),
            axis=1,
            keepdims=True,
        )
        for e in range(EXP_GROUP)
    )
    sigma = jax.nn.sigmoid(gate_pre)
    silu = gate_pre * sigma
    hidden = silu * up_pre
    dh = dh_raw * row_gate
    d_gate_pre = dh * up_pre * sigma * (1.0 + gate_pre * (1.0 - sigma))
    d_up_pre = dh * silu
    gate_term = jnp.sum(dh_raw * hidden, axis=1, keepdims=True)
    own = jnp.concatenate(
        [
            (hidden * row_gate).astype(BF16),
            d_gate_pre.astype(BF16),
            d_up_pre.astype(BF16),
            *in_parts(gate_term, 2),
        ],
        axis=1,
    )
    full = lax.all_gather(own, "col", axis=0, tiled=True)
    by_token = jnp.einsum("ert,rf->etf", pick_bf, full, preferred_element_type=F32).astype(BF16)
    hid, dgp, dup = by_token[:, :, :ff], by_token[:, :, ff : 2 * ff], by_token[:, :, 2 * ff : 3 * ff]
    mixed_part = jnp.einsum("etf,efd->td", hid, w_down, preferred_element_type=F32)
    dtok_part = jnp.einsum("etf,ekf->tk", dgp, w_gate, preferred_element_type=F32) + jnp.einsum(
        "etf,ekf->tk", dup, w_up, preferred_element_type=F32
    )
    term = by_token[:, :, 3 * ff].astype(F32) + by_token[:, :, 3 * ff + 1].astype(F32)
    term_k = jnp.sum(jnp.where(match, term.T[:, None, :], 0.0), axis=2)
    send = jnp.concatenate(
        [mixed_part.astype(BF16), dtok_part.astype(BF16), *in_parts(term_k, 2)], axis=1
    )
    peers = lax.axis_size(PLANE)
    back = lax.all_to_all(send.reshape(peers, -1, send.shape[1]), PLANE, 0, 0, tiled=True)
    grad_gate = jnp.einsum("td,etf->edf", tok_all, dgp, preferred_element_type=F32).astype(BF16)
    grad_up = jnp.einsum("td,etf->edf", tok_all, dup, preferred_element_type=F32).astype(BF16)
    grad_down = jnp.einsum("etf,td->efd", hid, cot_all, preferred_element_type=F32).astype(BF16)
    total = jnp.sum(back.astype(F32), axis=0)
    mixed = total[:, :width].astype(BF16)
    d_tokens = total[:, width : 2 * width].astype(BF16)
    d_gates = total[:, 2 * width : 2 * width + TOPK] + total[:, 2 * width + TOPK :]
    return mixed, d_tokens, d_gates, grad_gate, grad_up, grad_down


def local(tokens, cotangent, w_gate, w_up, w_down, expert_ids, gates):
    tok_all, cot_all, ids, weights = dispatched(tokens, cotangent, expert_ids, gates)
    count = ids.shape[0]
    here = ids - lax.axis_index("expert") * EXP_GROUP
    match = here[:, :, None] == jnp.arange(EXP_GROUP, dtype=jnp.int32)[None, None, :]
    used = jnp.any(match, axis=1)
    gate_of = jnp.sum(jnp.where(match, weights[:, :, None], 0.0), axis=1)
    order = jnp.arange(count, dtype=jnp.int32)
    before = (order[None, :] < order[:, None]).astype(BF16)
    ahead = jnp.sum(
        jnp.dot(before, used.astype(BF16), preferred_element_type=F32), axis=1, keepdims=True
    ).astype(jnp.int32)
    inner = jnp.cumsum(used.astype(jnp.int32), axis=1) - used.astype(jnp.int32)
    place = jnp.where(used, ahead + inner, -1)
    return routed(1024, tok_all, cot_all, match, gate_of, place, w_gate, w_up, w_down)


def solution(mesh):
    in_specs = (
        P(("expert", "row"), "col"),
        P(("expert", "row"), "col"),
        P("expert", "col", "row"),
        P("expert", "col", "row"),
        P("expert", "row", "col"),
        P(("expert", "row"), None),
        P(("expert", "row"), None),
    )
    out_specs = (
        P(("expert", "row"), "col"),
        P(("expert", "row"), "col"),
        P(("expert", "row"), None),
        P("expert", "col", "row"),
        P("expert", "col", "row"),
        P("expert", "row", "col"),
    )
    return jax.shard_map(local, mesh=mesh, in_specs=in_specs, out_specs=out_specs, check_vma=False)
```

time: 332 us -> 196 us (0.59)
  blocking collectives: 78.4 us -> 0 us
  waiting for transfers between devices: 157 us -> 101 us
  starting transfers between devices: 39.6 us -> 29.4 us
  matrix products: 17.7 us -> 27.3 us
    psum x1 -> x0, waiting for transfers between devices: 111 us -> none  [local(): lax.psum(jnp.einsum('med,efd->mef', dy_full, down_wide, precision=lax.Pre...]
    unnamed x1 -> x0, blocking collectives: 78.4 us -> none
    all_gather x0 -> x1, waiting for transfers between devices: none -> 37.1 us  [routed(): full = lax.all_gather(own, 'col', axis=0, tiled=True)]
    all_to_all x6 -> x3, waiting for transfers between devices: 46.3 us -> 64.3 us  [the longest x1 50.6 us: routed(): lax.all_to_all(parts.reshape(chunks, chunk, 3 * ff), 'col', 0, 0, tiled=T...]
    all_to_all x6 -> x3, starting transfers between devices: 39.6 us -> 29.1 us  [the longest x1 12.4 us: routed(): lax.all_to_all(send.reshape(peers, -1, send.shape[1]), PLANE, 0, 0, tiled...]
    dot_general x13 -> x12, matrix products: 17.7 us -> 27.3 us  [the longest x1 7.09 us: routed(): jnp.einsum('ert,rf->etf', pick_bf, full, preferred_element_type=F32)]
    concatenate x1 -> x6, local copies, waits for them, and re-layouts: 0.69 us -> 4.94 us  [the longest x1 2.56 us: routed(): jnp.concatenate([(hidden * row_gate).astype(BF16), d_gate_pre.astype(BF16...]
    unnamed x25 -> x29, local copies, waits for them, and re-layouts: 3.95 us -> 7.18 us
  transfers between devices with their start and end apart: 7 -> 4, of which waited for: 7 -> 3; matrix products, arithmetic and copies ran while one was open for 3% -> 9% of each run, Pallas kernels for 0% -> 0%
where the time goes in v1:
time: 196 us; the launch traced here: 195 us
  waiting for transfers between devices  101 us (52%)
  starting transfers between devices  29.4 us (15%)
  matrix products  27.3 us (14%)
  local copies, waits for them, and re-layouts  15.3 us (8%)
  between operations  14.5 us (7%)
  other arithmetic  7.57 us (4%)
    all_to_all x1, waiting for transfers between devices, routed(): lax.all_to_all(parts.reshape(chunks, chunk, 3 * ff), 'col', 0, 0, tiled=T...  50.6 us
    all_gather x1, waiting for transfers between devices, routed(): full = lax.all_gather(own, 'col', axis=0, tiled=True)  37.1 us
    all_to_all x1, waiting for transfers between devices, told_to_all(): lax.all_to_all(jnp.broadcast_to(value[None], (peers, *value.shape)), axis...  13.7 us
    all_to_all x1, starting transfers between devices, routed(): lax.all_to_all(send.reshape(peers, -1, send.shape[1]), PLANE, 0, 0, tiled...  12.4 us
    all_to_all x1, starting transfers between devices, told_to_all(): lax.all_to_all(jnp.broadcast_to(value[None], (peers, *value.shape)), axis...  8.58 us
    all_to_all x1, starting transfers between devices, routed(): lax.all_to_all(parts.reshape(chunks, chunk, 3 * ff), 'col', 0, 0, tiled=T...  8.17 us
    unnamed x29, local copies, waits for them, and re-layouts  7.18 us
    dot_general x1, matrix products, routed(): jnp.einsum('ert,rf->etf', pick_bf, full, preferred_element_type=F32)  7.09 us
  transfers between devices with their start and end apart: 4, of which 3 were waited for; matrix products, arithmetic and copies ran while one was open for 9% of the time, Pallas kernels for 0%

profile of v1, /device:TPU:1, one launch (start us, length us, event | category | flops | bytes accessed | tf_op | source)
XLA Modules:
  0.0 195.3 jit_solution(7876798032074627839)
XLA Ops:
  7.2 0.0 copy-start
  7.2 0.8 convert_element_type.115
  8.0 0.1 copy.81
  8.1 0.7 fusion.57
  8.7 0.1 copy.84
  8.8 0.1 copy.83
  8.9 0.1 copy.82
  9.0 0.8 concatenate.23
  9.9 0.9 broadcast_in_dim.90
  10.8 8.6 %all-to-all-start = ((bf16[32,16,736]{2,1,0:T(8,128)(2,1)}), bf16[32,16,736]{2,1,0:T(8,128)(2,1)S(1)}, u32[]{:S(2)}, u32[]{:S(2)}) async-start(bf16[32,16,736]{2,1,0:T(8,128)(2,1)} %broadcast_in_dim.90), calls=%async_computation | async-start | bytes 1572864 | tf_op jit(solution)/shard_map/all_to_all | solution.py:28
  19.4 13.7 %all-to-all-done = bf16[32,16,736]{2,1,0:T(8,128)(2,1)S(1)} async-done(((bf16[32,16,736]{2,1,0:T(8,128)(2,1)}), bf16[32,16,736]{2,1,0:T(8,128)(2,1)S(1)}, u32[]{:S(2)}, u32[]{:S(2)}) %all-to-all-start) | async-done | bytes 753696 | tf_op jit(solution)/shard_map/all_to_all | solution.py:28
  33.1 0.1 slice.123
  33.2 0.1 copy.104
  33.4 0.3 convolution_reduce_fusion
  33.7 0.7 iota_compare_fusion
  34.5 0.0 copy-start.3
  34.5 0.0 copy-start.4
  34.5 0.7 iota_compare_fusion.2
  35.3 0.0 copy-start.5
  35.3 0.0 copy-start.6
  35.3 0.0 copy-start.10
  35.3 3.5 %convolution_convert_fusion.1 = bf16[4,1024,720]{1,2,0:T(8,128)(2,1)S(1)} fusion(bf16[512,736]{1,0:T(8,128)(2,1)S(1)} %bitcast.89, pred[1,1024,512]{2,1,0:T(32,128)(4,1)S(1)} %get-tuple-element.61, pred[1,1024,512]{2,1,0:T(32,128)(4,1)S(1)} %get-tuple-element.62, pred[1,1024,512]{2,1,0:T(32,128)(4,1)S(1)} %get-tuple-element.63, ...), kind=kOutput, calls=%fused_computation.3 | convolution fusion | flops 3029139456 | bytes 8749056 | tf_op jit(solution)/shard_map/ert,td->erd/dot_general | solution.py:54
  38.8 0.0 copy-done.1
  38.9 1.4 fusion.27
  40.3 0.1 copy.116
  40.4 0.0 copy-start.8
  40.4 1.3 fusion.30
  41.8 1.4 fusion.24
  43.2 0.1 copy.117
  43.3 0.1 copy.115
  43.5 1.5 pad_maximum_fusion
  45.0 8.2 %all-to-all-start.1 = ((bf16[8,128,1080]{1,2,0:T(8,128)(2,1)}), bf16[8,128,1080]{1,2,0:T(8,128)(2,1)S(1)}, u32[]{:S(2)}, u32[]{:S(2)}) async-start(bf16[8,128,1080]{1,2,0:T(8,128)(2,1)} %pad_maximum_fusion), calls=%async_computation.1 | async-start | bytes 4423680 | tf_op jit(solution)/shard_map/all_to_all | solution.py:61
  53.2 0.2 all-gather.2.cloned.1.call-start
  53.4 1.0 slice_convert_fusion
  54.4 0.9 slice_add_fusion
  55.3 1.1 copy.92
  56.4 0.2 select_reduce_fusion.2
  56.7 50.6 %all-to-all-done.1 = bf16[8,128,1080]{1,2,0:T(8,128)(2,1)S(1)} async-done(((bf16[8,128,1080]{1,2,0:T(8,128)(2,1)}), bf16[8,128,1080]{1,2,0:T(8,128)(2,1)S(1)}, u32[]{:S(2)}, u32[]{:S(2)}) %all-to-all-start.1) | async-done | bytes 2211872 | tf_op jit(solution)/shard_map/all_to_all | solution.py:61
  107.3 0.3 convert_reduce_fusion
  107.6 0.2 multiply_convert_fusion
  107.8 2.6 %concatenate.29 = bf16[128,1082]{0,1:T(8,128)(2,1)} concatenate(bf16[128,360]{0,1:T(8,128)(2,1)S(1)} %get-tuple-element.41, bf16[128,360]{0,1:T(8,128)(2,1)S(1)} %get-tuple-element.42, bf16[128,360]{0,1:T(8,128)(2,1)S(1)} %get-tuple-element.40, bf16[128,1]{0,1:T(2,128)(2,1)S(1)} %get-tuple-element.60, bf16[128,1]{0,1:T(2,128)(2,1)S(1)} %get-tuple-element.59), dimensions={1} | concatenate | bytes 553984 | tf_op jit(solution)/shard_map/concatenate | solution.py:80
  110.4 0.0 all-gather.2.cloned.1.call-update
  110.4 37.1 %all-gather.2.cloned.1.call-done = bf16[1024,1082]{0,1:T(8,128)(2,1)} async-done(((bf16[128,1082]{0,1:T(8,128)(2,1)}), bf16[1024,1082]{0,1:T(8,128)(2,1)}) %all-gather.2.cloned.1.call-update) | async-done | bytes 2215952 | tf_op jit(solution)/shard_map/all_gather | solution.py:89
  147.4 7.1 %convolution_convert_fusion = bf16[4,512,1082]{1,2,0:T(8,128)(2,1)S(1)} fusion(bf16[1024,1082]{0,1:T(8,128)(2,1)} %all-gather.2.cloned.1.call-done, pred[1,1024,512]{2,1,0:T(32,128)(4,1)} %copy-done.3, pred[1,1024,512]{2,1,0:T(32,128)(4,1)} %copy-done.4, pred[1,1024,512]{2,1,0:T(32,128)(4,1)} %copy-done.5, pred[1,1024,512]{2,1,0:T(32,128)(4,1)} %copy-done.6), kind=kOutput, calls=%fused_computation.1 | convolution fusion | flops 4546744320 | bytes 8744960 | tf_op jit(solution)/shard_map/ert,rf->etf/dot_general | solution.py:90
  154.6 0.0 copy-start.9
  154.6 0.8 fusion.45
  155.4 1.3 copy-done.9
  156.7 0.8 fusion.36
  157.5 0.4 copy-done.11
  157.9 0.7 fusion.48
  158.6 0.0 copy-start.2
  158.7 0.1 pad_maximum_fusion.1
  158.7 1.2 copy.94
  159.9 12.4 %all-to-all-start.2 = ((bf16[32,16,728]{2,1,0:T(8,128)(2,1)}), bf16[32,16,728]{2,1,0:T(8,128)(2,1)S(1)}, u32[]{:S(2)}, u32[]{:S(2)}) async-start(bf16[32,16,728]{2,1,0:T(8,128)(2,1)} %bitcast.19), calls=%async_computation.2 | async-start | bytes 1572864 | tf_op jit(solution)/shard_map/all_to_all | solution.py:102
  172.3 3.3 %fusion.13 = bf16[4,360,360]{1,2,0:T(8,128)(2,1)} fusion(bf16[4,512,1082]{1,2,0:T(8,128)(2,1)} %copy-done.7, bf16[512,736]{1,0:T(8,128)(2,1)S(1)} %bitcast.91), kind=kOutput, calls=%fused_computation.23 | convolution fusion | flops 531360000 | bytes 2904576 | tf_op jit(solution)/shard_map/td,etf->edf/dot_general | solution.py:103
  175.6 2.3 %copy.98 = bf16[4,360,360]{2,1,0:T(8,128)(2,1)} copy(bf16[4,360,360]{1,2,0:T(8,128)(2,1)} %fusion.13) | data formatting | bytes 2073600
  177.9 3.3 %fusion.14 = bf16[4,360,360]{1,2,0:T(8,128)(2,1)} fusion(bf16[4,512,1082]{1,2,0:T(8,128)(2,1)} %copy-done.7, bf16[512,736]{1,0:T(8,128)(2,1)S(1)} %bitcast.92), kind=kOutput, calls=%fused_computation.24 | convolution fusion | flops 531360000 | bytes 2904576 | tf_op jit(solution)/shard_map/td,etf->edf/dot_general | solution.py:104
  181.2 2.3 %copy.99 = bf16[4,360,360]{2,1,0:T(8,128)(2,1)} copy(bf16[4,360,360]{1,2,0:T(8,128)(2,1)} %fusion.14) | data formatting | bytes 2073600
  183.6 3.4 %convolution_convert_fusion.2 = bf16[4,360,360]{2,1,0:T(8,128)(2,1)} fusion(bf16[4,512,1082]{1,2,0:T(8,128)(2,1)} %copy-done.7, bf16[512,736]{1,0:T(8,128)(2,1)S(1)} %bitcast.93), kind=kOutput, calls=%fused_computation.17 | convolution fusion | flops 531360000 | bytes 2904576 | tf_op jit(solution)/shard_map/etf,td->efd/dot_general | solution.py:105
  186.9 0.0 all-to-all-done.2
  187.0 0.1 convert_reduce_fusion.1
  187.1 0.1 slice_add_fusion.2
  187.2 0.7 copy.97
  187.8 0.7 fusion.60
  (29 shorter events, 0.2 us)
Async XLA Ops:
  7.2 33.3 %copy-start = (bf16[4,360,360]{2,1,0:T(8,128)(2,1)S(1)}, bf16[4,360,360]{2,1,0:T(8,128)(2,1)}, u32[]{:S(2)}) copy-start(bf16[4,360,360]{2,1,0:T(8,128)(2,1)} %param.11) | copy-start | bytes 3110404
  10.8 22.3 %all-to-all-start = ((bf16[32,16,736]{2,1,0:T(8,128)(2,1)}), bf16[32,16,736]{2,1,0:T(8,128)(2,1)S(1)}, u32[]{:S(2)}, u32[]{:S(2)}) async-start(bf16[32,16,736]{2,1,0:T(8,128)(2,1)} %broadcast_in_dim.90), calls=%async_computation | async-start | bytes 1572864 | tf_op jit(solution)/shard_map/all_to_all | solution.py:28
  33.1 5.7 %copy-start.1 = (bf16[32,16,736]{2,1,0:T(8,128)(2,1)}, bf16[32,16,736]{2,1,0:T(8,128)(2,1)S(1)}, u32[]{:S(2)}) copy-start(bf16[32,16,736]{2,1,0:T(8,128)(2,1)S(1)} %all-to-all-done) | copy-start | bytes 2260996
  34.5 4.4 %copy-start.3 = (pred[1,1024,512]{2,1,0:T(32,128)(4,1)}, pred[1,1024,512]{2,1,0:T(32,128)(4,1)S(1)}, u32[]{:S(2)}) copy-start(pred[1,1024,512]{2,1,0:T(32,128)(4,1)S(1)} %get-tuple-element.61) | copy-start | bytes 1572868
  34.5 4.4 %copy-start.4 = (pred[1,1024,512]{2,1,0:T(32,128)(4,1)}, pred[1,1024,512]{2,1,0:T(32,128)(4,1)S(1)}, u32[]{:S(2)}) copy-start(pred[1,1024,512]{2,1,0:T(32,128)(4,1)S(1)} %get-tuple-element.62) | copy-start | bytes 1572868
  35.3 3.6 %copy-start.5 = (pred[1,1024,512]{2,1,0:T(32,128)(4,1)}, pred[1,1024,512]{2,1,0:T(32,128)(4,1)S(1)}, u32[]{:S(2)}) copy-start(pred[1,1024,512]{2,1,0:T(32,128)(4,1)S(1)} %get-tuple-element.63) | copy-start | bytes 1572868
  35.3 3.6 %copy-start.6 = (pred[1,1024,512]{2,1,0:T(32,128)(4,1)}, pred[1,1024,512]{2,1,0:T(32,128)(4,1)S(1)}, u32[]{:S(2)}) copy-start(pred[1,1024,512]{2,1,0:T(32,128)(4,1)S(1)} %get-tuple-element.64) | copy-start | bytes 1572868
  35.3 3.6 %copy-start.10 = (bf16[4,360,360]{2,1,0:T(8,128)(2,1)S(1)}, bf16[4,360,360]{2,1,0:T(8,128)(2,1)}, u32[]{:S(2)}) copy-start(bf16[4,360,360]{2,1,0:T(8,128)(2,1)} %param.10) | copy-start | bytes 3110404
  40.4 1.4 copy-start.8
  45.0 62.3 %all-to-all-start.1 = ((bf16[8,128,1080]{1,2,0:T(8,128)(2,1)}), bf16[8,128,1080]{1,2,0:T(8,128)(2,1)S(1)}, u32[]{:S(2)}, u32[]{:S(2)}) async-start(bf16[8,128,1080]{1,2,0:T(8,128)(2,1)} %pad_maximum_fusion), calls=%async_computation.1 | async-start | bytes 4423680 | tf_op jit(solution)/shard_map/all_to_all | solution.py:61
  53.2 94.3 %all-gather.2.cloned.1.call-start = ((), (), s32[]{:S(2)}) async-start(), calls=%async_computation.3 | async-start | bytes 2506752 | tf_op jit(solution)/shard_map/all_gather | solution.py:89
  154.5 3.0 %copy-start.7 = (bf16[4,512,1082]{1,2,0:T(8,128)(2,1)}, bf16[4,512,1082]{1,2,0:T(8,128)(2,1)S(1)}, u32[]{:S(2)}) copy-start(bf16[4,512,1082]{1,2,0:T(8,128)(2,1)S(1)} %convolution_convert_fusion) | copy-start | bytes 13295620
  154.6 2.1 %copy-start.9 = (bf16[4,360,360]{2,1,0:T(8,128)(2,1)S(1)}, bf16[4,360,360]{2,1,0:T(8,128)(2,1)}, u32[]{:S(2)}) copy-start(bf16[4,360,360]{2,1,0:T(8,128)(2,1)} %param.9) | copy-start | bytes 3110404
  156.7 1.2 copy-start.11
  158.6 13.6 %copy-start.2 = (bf16[32,16,736]{2,1,0:T(8,128)(2,1)S(1)}, bf16[32,16,736]{2,1,0:T(8,128)(2,1)}, u32[]{:S(2)}) copy-start(bf16[32,16,736]{2,1,0:T(8,128)(2,1)} %copy-done.1) | copy-start | bytes 2260996
  159.9 27.1 %all-to-all-start.2 = ((bf16[32,16,728]{2,1,0:T(8,128)(2,1)}), bf16[32,16,728]{2,1,0:T(8,128)(2,1)S(1)}, u32[]{:S(2)}, u32[]{:S(2)}) async-start(bf16[32,16,728]{2,1,0:T(8,128)(2,1)} %bitcast.19), calls=%async_computation.2 | async-start | bytes 1572864 | tf_op jit(solution)/shard_map/all_to_all | solution.py:102
Sparse Core Ops, SparseCore 0:
  110.5 36.8 all-gather.1
